TPU v7x, 32 devices: a whole 2x2x4 slice. The times are simulated.
32 devices in a mesh: groups: 2 (over x), chan: 16 (over z, y, core).
Axes of the slice: x: 2, y: 2, z: 4, core: 2. Of those that a mesh axis runs over, the one named last changes fastest.
Arguments:
- spectra: bfloat16 [2, 8, 512, 512], P(None, 'groups', 'chan'), parts along dimension 1, may hold values from -6 to 6
- filter_bank: float32 [2, 8, 65], replicated, may hold values from -0.5 to 0.5
- band_index: int32 [512], replicated, may hold values from 0 to 7
- window_mask: int32 [8, 512], P('groups', 'chan'), parts along dimension 0, may hold values 0 or 1
- owner_order: int32 [8], P('groups'), parts along dimension 0, may hold values from 0 to 15, as said below
- source_offset: int32 [8, 32], P('groups'), parts along dimension 0, may hold values from 0 to 31, each once within a row
Outputs:
- cross: bfloat16 [2, 256, 512, 512], P(None, 'groups', 'chan'), parts along dimension 1
There are 2 independent parts, one for each index of `groups`. A program takes and returns all parts, laid end to end along the dimension named above; an argument that names none is the same for every part. Nothing has to cross between parts.
Inputs may be any that keep to these rules, and one draw needn't show every extreme that they name: `owner_order`: 4 distinct device indices, below 16.
All inputs are finite; a program needn't handle non-finite values. No bound on the sum of `window_mask` on one device may be relied on, other than what follows from the above.
Results may differ from a plain program's by a relative error of at most 0.0057.
Values may be sent and summed in bfloat16 or wider, within the bound.
A program may use at most 192 MiB of HBM per device.

v0:
```python
import jax
import jax.numpy as jnp
from jax import lax
from jax.sharding import PartitionSpec as P

WIN = 4
TAPS = 65
NBANK = 8
SMOOTH = 17
ROUNDS = 4
water_level = 0.05


def padded_2(cells, sides, width):
    for axis, dim in sides:
        count = lax.axis_size(axis)
        ends = count - 1
        head = lax.slice_in_dim(cells, 0, width, axis=dim)
        tail = lax.slice_in_dim(cells, cells.shape[dim] - width, cells.shape[dim], axis=dim)
        cells = jnp.concatenate(
            [
                lax.ppermute(tail, axis, [(i, (i + 1) % count) for i in range(ends)]),
                cells,
                lax.ppermute(head, axis, [((i + 1) % count, i) for i in range(ends)]),
            ],
            axis=dim,
        )
    return cells


def filter_taps(filter_bank, band_index):
    choose = (band_index[:, None] == jnp.arange(NBANK, dtype=jnp.int32)[None, :]).astype(
        jnp.float32
    )
    return jnp.einsum("fb,pbk->pkf", choose, filter_bank, precision=lax.Precision.HIGHEST)


def velocity_whiten(padded, taps, window_mask):
    count = padded.shape[2] - (TAPS - 1)
    out_pos = jnp.arange(count, dtype=jnp.int32)
    in_pos = jnp.arange(padded.shape[2], dtype=jnp.int32)
    tap_pos = jnp.arange(TAPS, dtype=jnp.int32)
    shifter = (in_pos[None, :, None] - out_pos[:, None, None] == tap_pos[None, None, :]).astype(
        jnp.float32
    )
    banded = jnp.einsum("okt,ptf->pfok", shifter, taps, precision=lax.Precision.HIGHEST)
    products = jnp.einsum("pfok,qwkf->pqwof", banded, padded, precision=lax.Precision.HIGHEST)
    real_sum = products[0, 0] - products[1, 1]
    imag_sum = products[0, 1] + products[1, 0]
    power = real_sum * real_sum + imag_sum * imag_sum
    reach = SMOOTH // 2
    bins = jnp.arange(power.shape[2], dtype=jnp.int32)
    window_band = (jnp.abs(bins[:, None] - bins[None, :]) <= reach).astype(jnp.float32)
    smooth = jnp.einsum("wcg,gf->wcf", power, window_band, precision=lax.Precision.HIGHEST) / SMOOTH
    scale = lax.rsqrt(smooth + water_level) * window_mask.astype(jnp.float32)[:, :, None]
    return jnp.stack([real_sum * scale, imag_sum * scale]).astype(jnp.bfloat16)


def cross_block(source, whitened, swapped):
    real_out = jnp.einsum("pwsf,pwcf->scf", source, whitened, preferred_element_type=jnp.float32)
    imag_out = jnp.einsum("pwsf,pwcf->scf", source, swapped, preferred_element_type=jnp.float32)
    return (jnp.stack([real_out, imag_out]) / WIN).astype(jnp.bfloat16)


def body(spectra, filter_bank, band_index, window_mask, owner_order, source_offset):
    half_width = TAPS // 2
    padded = padded_2(spectra, (("chan", 2),), half_width)
    taps = filter_taps(filter_bank, band_index)
    whitened = velocity_whiten(padded.astype(jnp.float32), taps, window_mask)
    swapped = jnp.stack([whitened[1], -whitened[0]])
    positions = jnp.arange(whitened.shape[2], dtype=jnp.int32)

    def own_sources(round_pos):
        choose = (source_offset[round_pos][:, None] == positions[None, :]).astype(jnp.bfloat16)
        picked = jnp.einsum("sc,pwcf->pwsf", choose, whitened, preferred_element_type=jnp.float32)
        return picked.astype(jnp.bfloat16)

    blocks = []
    device_here = lax.axis_index("chan")
    nothing = jnp.zeros((), jnp.float32)
    stacked = jnp.stack(
        [
            jnp.where(
                device_here == owner_order[round_pos],
                own_sources(round_pos).astype(jnp.float32),
                nothing,
            )
            for round_pos in range(ROUNDS)
        ]
    )
    summed = lax.psum(stacked, "chan").astype(jnp.bfloat16)
    for round_pos in range(ROUNDS):
        blocks.append(cross_block(summed[round_pos], whitened, swapped))
    return jnp.concatenate(blocks, axis=1)


def solution(mesh):
    in_specs = (
        P(None, "groups", "chan", None),
        P(),
        P(),
        P("groups", "chan"),
        P("groups"),
        P("groups", None),
    )
    out_specs = P(None, "groups", "chan", None)
    return jax.shard_map(body, mesh=mesh, in_specs=in_specs, out_specs=out_specs, check_vma=False)
```

profile of v0, /device:TPU:0, one launch (start us, length us, event | category | flops | bytes accessed | tf_op | source)
XLA Modules:
  0.0 280.7 jit_solution(10334228674612800739)
XLA Ops:
  0.0 2.5 collective-permute-start
  4.9 8.0 %convolution_bitcast_fusion = f32[2,512,32,96,1]{1,3,2,0,4:T(8,128)} fusion(f32[2,65,512,1]{2,1,3,0:T(8,128)S(1)} %convolution_bitcast_fusion.10, s32[32,96]{1,0:T(8,128)S(1)} %iota_subtract_fusion), kind=kOutput, calls=%fused_computation.1 | convolution fusion | flops 2453867520 | bytes 12861440 | tf_op jit(solution)/shard_map/okt,ptf->pfok/dot_general | solution.py:46
  14.3 18.0 %copy.108 = f32[2,512,32,96,1]{3,2,0,4,1:T(8,128)} copy(f32[2,512,32,96,1]{1,3,2,0,4:T(8,128)} %convolution_bitcast_fusion) | data formatting | bytes 25165824 | tf_op jit(solution)/shard_map/okt,ptf->pfok/dot_general | solution.py:46
  36.4 49.4 %convolution_bitcast_fusion.9 = f32[2,2,4,32,512]{3,2,0,1,4:T(4,128)} fusion(f32[2,512,32,96,1]{3,2,0,4,1:T(8,128)} %copy.108, bf16[2,4,32,512]{2,1,0,3:T(4,128)(2,1)S(1)} %copy.72, bf16[2,4,32,512]{2,1,0,3:T(4,128)(2,1)S(1)} %copy.71, bf16[2,4,32,512]{2,1,0,3:T(4,128)(2,1)S(1)} %copy.70), kind=kOutput, calls=%fused_computation.18 | convolution fusion | flops 304349184 | bytes 14417920 | tf_op jit(solution)/shard_map/pfok,qwkf->pqwof/dot_general | solution.py:47
  85.8 2.7 multiply_add_fusion
  100.5 78.1 %all-reduce.1 = bf16[4,2,4,32,512]{4,3,2,1,0:T(8,128)(2,1)S(1)} all-reduce(f32[4,2,4,32,512]{4,3,2,1,0:T(8,128)} %pad_maximum_fusion.1), channel_id=1, replica_groups=mesh['groups'=2,'chan'=16] {'chan'}, use_global_device_ids=true, to_apply=%region_0.1 | all-reduce | flops 524288 | bytes 3145728 | tf_op jit(solution)/shard_map/psum | solution.py:91
  181.0 4.3 %convolution_bitcast_fusion.6 = f32[1,32,32,512]{1,2,3,0:T(8,128)} fusion(bf16[2,4,32,512]{2,1,3,0:T(4,128)(2,1)S(1)} %copy.118, bf16[1,4,32,512]{2,1,3,0:T(4,128)(2,1)S(1)} %fusion.32, bf16[1,4,32,512]{2,1,3,0:T(4,128)(2,1)S(1)} %get-tuple-element.6), kind=kOutput, calls=%fused_computation.15 | convolution fusion | flops 8912896 | bytes 2621440 | tf_op jit(solution)/shard_map/pwsf,pwcf->scf/dot_general | solution.py:60
  185.3 4.3 %convolution_bitcast_fusion.5 = f32[1,32,32,512]{1,2,3,0:T(8,128)} fusion(bf16[2,4,32,512]{2,1,3,0:T(4,128)(2,1)S(1)} %copy.118, bf16[1,4,32,512]{2,1,3,0:T(4,128)(2,1)S(1)} %get-tuple-element.5, bf16[1,4,32,512]{2,1,3,0:T(4,128)(2,1)S(1)} %fusion.32), kind=kOutput, calls=%fused_computation.14 | convolution fusion | flops 8912896 | bytes 2621440 | tf_op jit(solution)/shard_map/pwsf,pwcf->scf/dot_general | solution.py:61
  190.3 4.3 %convolution_bitcast_fusion.8 = f32[1,32,32,512]{1,2,3,0:T(8,128)} fusion(bf16[2,4,32,512]{2,1,3,0:T(4,128)(2,1)S(1)} %copy.114, bf16[1,4,32,512]{2,1,3,0:T(4,128)(2,1)S(1)} %fusion.32, bf16[1,4,32,512]{2,1,3,0:T(4,128)(2,1)S(1)} %get-tuple-element.6), kind=kOutput, calls=%fused_computation.17 | convolution fusion | flops 8912896 | bytes 2621440 | tf_op jit(solution)/shard_map/pwsf,pwcf->scf/dot_general | solution.py:60
  194.6 4.3 %convolution_bitcast_fusion.7 = f32[1,32,32,512]{1,2,3,0:T(8,128)} fusion(bf16[2,4,32,512]{2,1,3,0:T(4,128)(2,1)S(1)} %copy.114, bf16[1,4,32,512]{2,1,3,0:T(4,128)(2,1)S(1)} %get-tuple-element.5, bf16[1,4,32,512]{2,1,3,0:T(4,128)(2,1)S(1)} %fusion.32), kind=kOutput, calls=%fused_computation.16 | convolution fusion | flops 8912896 | bytes 2621440 | tf_op jit(solution)/shard_map/pwsf,pwcf->scf/dot_general | solution.py:61
  199.6 4.3 %convolution_bitcast_fusion.2 = f32[1,32,32,512]{1,2,3,0:T(8,128)} fusion(bf16[2,4,32,512]{2,1,3,0:T(4,128)(2,1)S(1)} %copy.126, bf16[1,4,32,512]{2,1,3,0:T(4,128)(2,1)S(1)} %fusion.32, bf16[1,4,32,512]{2,1,3,0:T(4,128)(2,1)S(1)} %get-tuple-element.6), kind=kOutput, calls=%fused_computation.11 | convolution fusion | flops 8912896 | bytes 2621440 | tf_op jit(solution)/shard_map/pwsf,pwcf->scf/dot_general | solution.py:60
  203.9 4.3 %convolution_bitcast_fusion.1 = f32[1,32,32,512]{1,2,3,0:T(8,128)} fusion(bf16[2,4,32,512]{2,1,3,0:T(4,128)(2,1)S(1)} %copy.126, bf16[1,4,32,512]{2,1,3,0:T(4,128)(2,1)S(1)} %get-tuple-element.5, bf16[1,4,32,512]{2,1,3,0:T(4,128)(2,1)S(1)} %fusion.32), kind=kOutput, calls=%fused_computation.10 | convolution fusion | flops 8912896 | bytes 2621440 | tf_op jit(solution)/shard_map/pwsf,pwcf->scf/dot_general | solution.py:61
  208.9 4.3 %convolution_bitcast_fusion.4 = f32[1,32,32,512]{1,2,3,0:T(8,128)} fusion(bf16[2,4,32,512]{2,1,3,0:T(4,128)(2,1)S(1)} %copy.122, bf16[1,4,32,512]{2,1,3,0:T(4,128)(2,1)S(1)} %fusion.32, bf16[1,4,32,512]{2,1,3,0:T(4,128)(2,1)S(1)} %get-tuple-element.6), kind=kOutput, calls=%fused_computation.13 | convolution fusion | flops 8912896 | bytes 2621440 | tf_op jit(solution)/shard_map/pwsf,pwcf->scf/dot_general | solution.py:60
  213.2 4.5 %convolution_bitcast_fusion.3 = f32[1,32,32,512]{1,2,3,0:T(8,128)} fusion(bf16[2,4,32,512]{2,1,3,0:T(4,128)(2,1)S(1)} %copy.122, bf16[1,4,32,512]{2,1,3,0:T(4,128)(2,1)S(1)} %get-tuple-element.5, bf16[1,4,32,512]{2,1,3,0:T(4,128)(2,1)S(1)} %fusion.32), kind=kOutput, calls=%fused_computation.12 | convolution fusion | flops 8912896 | bytes 2621440 | tf_op jit(solution)/shard_map/pwsf,pwcf->scf/dot_general | solution.py:61
  217.7 5.8 %copy.92 = f32[1,32,32,512]{3,2,1,0:T(8,128)S(1)} copy(f32[1,32,32,512]{1,2,3,0:T(8,128)} %convolution_bitcast_fusion.6) | data formatting | bytes 4194304 | tf_op jit(solution)/shard_map/stack | solution.py:62
  223.5 6.6 %copy.93 = f32[1,32,32,512]{3,2,1,0:T(8,128)} copy(f32[1,32,32,512]{1,2,3,0:T(8,128)} %convolution_bitcast_fusion.5) | data formatting | bytes 4194304 | tf_op jit(solution)/shard_map/stack | solution.py:62
  230.1 6.6 %copy.86 = f32[1,32,32,512]{3,2,1,0:T(8,128)} copy(f32[1,32,32,512]{1,2,3,0:T(8,128)} %convolution_bitcast_fusion.8) | data formatting | bytes 4194304 | tf_op jit(solution)/shard_map/stack | solution.py:62
  236.7 6.6 %copy.87 = f32[1,32,32,512]{3,2,1,0:T(8,128)} copy(f32[1,32,32,512]{1,2,3,0:T(8,128)} %convolution_bitcast_fusion.7) | data formatting | bytes 4194304 | tf_op jit(solution)/shard_map/stack | solution.py:62
  243.4 6.6 %copy.104 = f32[1,32,32,512]{3,2,1,0:T(8,128)} copy(f32[1,32,32,512]{1,2,3,0:T(8,128)} %convolution_bitcast_fusion.2) | data formatting | bytes 4194304 | tf_op jit(solution)/shard_map/stack | solution.py:62
  250.0 6.7 %copy.105 = f32[1,32,32,512]{3,2,1,0:T(8,128)} copy(f32[1,32,32,512]{1,2,3,0:T(8,128)} %convolution_bitcast_fusion.1) | data formatting | bytes 4194304 | tf_op jit(solution)/shard_map/stack | solution.py:62
  256.7 6.6 %copy.98 = f32[1,32,32,512]{3,2,1,0:T(8,128)} copy(f32[1,32,32,512]{1,2,3,0:T(8,128)} %convolution_bitcast_fusion.4) | data formatting | bytes 4194304 | tf_op jit(solution)/shard_map/stack | solution.py:62
  263.3 6.6 %copy.99 = f32[1,32,32,512]{3,2,1,0:T(8,128)} copy(f32[1,32,32,512]{1,2,3,0:T(8,128)} %convolution_bitcast_fusion.3) | data formatting | bytes 4194304 | tf_op jit(solution)/shard_map/stack | solution.py:62
  269.9 3.6 %fusion = (bf16[2,32,32,512]{3,2,1,0:T(8,128)(2,1)S(1)}, bf16[2,32,32,512]{3,2,1,0:T(8,128)(2,1)S(1)}) fusion(f32[1,32,32,512]{3,2,1,0:T(8,128)} %copy.87, f32[1,32,32,512]{3,2,1,0:T(8,128)} %copy.86, f32[1,32,32,512]{3,2,1,0:T(8,128)} %copy.93, f32[1,32,32,512]{3,2,1,0:T(8,128)S(1)} %copy.92), kind=kLoop, calls=%fused_computation.3 | loop fusion | flops 6291456 | bytes 12582912 | tf_op jit(solution)/shard_map/convert_element_type | solution.py:62
  276.6 3.9 %pad_maximum_fusion = bf16[2,128,32,512]{3,2,1,0:T(8,128)(2,1)} fusion(bf16[2,32,32,512]{3,2,1,0:T(8,128)(2,1)S(1)} %get-tuple-element.22, bf16[2,32,32,512]{3,2,1,0:T(8,128)(2,1)S(1)} %get-tuple-element.21, bf16[2,32,32,512]{3,2,1,0:T(8,128)(2,1)S(1)} %get-tuple-element.20, bf16[2,32,32,512]{3,2,1,0:T(8,128)(2,1)S(1)} %get-tuple-element.19), kind=kLoop, calls=%fused_computation | loop fusion | flops 12582912 | bytes 16777216 | tf_op jit(solution)/shard_map/concatenate | solution.py:94
  (48 shorter events, 24.6 us)
Async XLA Ops:
  0.0 3.9 %copy-start = (f32[2,8,65]{2,1,0:T(8,128)S(1)}, f32[2,8,65]{2,1,0:T(8,128)}, u32[]{:S(2)}) copy-start(f32[2,8,65]{2,1,0:T(8,128)} %param.7) | copy-start | bytes 12484
  0.0 35.0 %collective-permute-start = (bf16[2,4,32,512]{3,2,1,0:T(8,128)(2,1)}, bf16[2,4,32,512]{3,2,1,0:T(8,128)(2,1)S(1)}, u32[]{:S(2)}, u32[]{:S(2)}) collective-permute-start(bf16[2,4,32,512]{3,2,1,0:T(8,128)(2,1)} %param.6), channel_id=1, source_target_pairs={{0,1},{1,2},{2,3},{3,4},{4,5},{5,6},{6,7},{7,8},{8,9},{9,10},{10,1... | collective-permute-start | bytes 786440 | tf_op jit(solution)/shard_map/ppermute | solution.py:22
  2.5 33.2 %collective-permute-start.1 = (bf16[2,4,32,512]{3,2,1,0:T(8,128)(2,1)}, bf16[2,4,32,512]{3,2,1,0:T(8,128)(2,1)S(1)}, u32[]{:S(2)}, u32[]{:S(2)}) collective-permute-start(bf16[2,4,32,512]{3,2,1,0:T(8,128)(2,1)} %param.6), channel_id=1, source_target_pairs={{1,0},{2,1},{3,2},{4,3},{5,4},{6,5},{7,6},{8,7},{9,8},{10,9},{11,1... | collective-permute-start | bytes 786440 | tf_op jit(solution)/shard_map/ppermute | solution.py:24
  4.9 8.0 %copy-start.7 = (s32[4]{0:T(128)S(1)}, s32[4]{0:T(128)}, u32[]{:S(2)}) copy-start(s32[4]{0:T(128)} %param.10) | copy-start | bytes 52
  4.9 8.7 %copy-start.6 = (bf16[2,4,32,512]{3,2,1,0:T(8,128)(2,1)S(1)}, bf16[2,4,32,512]{3,2,1,0:T(8,128)(2,1)}, u32[]{:S(2)}) copy-start(bf16[2,4,32,512]{3,2,1,0:T(8,128)(2,1)} %param.6) | copy-start | bytes 786436
  14.3 18.1 %copy-start.8 = (s32[4,32]{1,0:T(4,128)S(1)}, s32[4,32]{1,0:T(4,128)}, u32[]{:S(2)}) copy-start(s32[4,32]{1,0:T(4,128)} %param.9) | copy-start | bytes 1540
  14.3 20.7 %copy-start.9 = (s32[4,32]{1,0:T(4,128)S(1)}, s32[4,32]{1,0:T(4,128)}, u32[]{:S(2)}) copy-start(s32[4,32]{1,0:T(4,128)} %param.11) | copy-start | bytes 1540
  269.9 3.6 %copy-start.2 = (f32[1,32,32,512]{3,2,1,0:T(8,128)S(1)}, f32[1,32,32,512]{3,2,1,0:T(8,128)}, u32[]{:S(2)}) copy-start(f32[1,32,32,512]{3,2,1,0:T(8,128)} %copy.104) | copy-start | bytes 6291460
  269.9 4.1 %copy-start.3 = (f32[1,32,32,512]{3,2,1,0:T(8,128)S(1)}, f32[1,32,32,512]{3,2,1,0:T(8,128)}, u32[]{:S(2)}) copy-start(f32[1,32,32,512]{3,2,1,0:T(8,128)} %copy.105) | copy-start | bytes 6291460
  269.9 4.7 %copy-start.4 = (f32[1,32,32,512]{3,2,1,0:T(8,128)S(1)}, f32[1,32,32,512]{3,2,1,0:T(8,128)}, u32[]{:S(2)}) copy-start(f32[1,32,32,512]{3,2,1,0:T(8,128)} %copy.98) | copy-start | bytes 6291460
  269.9 5.3 %copy-start.5 = (f32[1,32,32,512]{3,2,1,0:T(8,128)S(1)}, f32[1,32,32,512]{3,2,1,0:T(8,128)}, u32[]{:S(2)}) copy-start(f32[1,32,32,512]{3,2,1,0:T(8,128)} %copy.99) | copy-start | bytes 6291460
  276.6 3.9 %copy-start.1 = (f32[2,8,65]{2,1,0:T(8,128)S(1)}, f32[2,8,65]{2,1,0:T(8,128)}, u32[]{:S(2)}) copy-start(f32[2,8,65]{2,1,0:T(8,128)} %param.7) | copy-start | bytes 12484
where the time goes:
time: 285 us; the launch traced here: 281 us
  matrix products  95.1 us (33%)
  local copies, waits for them, and re-layouts  81.1 us (28%)
  blocking collectives  78.1 us (27%)
  other arithmetic  19.4 us (7%)
  starting transfers between devices  3.83 us (1%)
  between operations  3.13 us (1%)
    psum x1, blocking collectives, body(): summed = lax.psum(stacked, 'chan').astype(jnp.bfloat16)  78.1 us
    another operation x8, local copies, waits for them, and re-layouts, cross_block(): return (jnp.stack([real_out, imag_out]) / WIN).astype(jnp.bfloat16)  52.2 us
    dot_general x1, matrix products, velocity_whiten(): jnp.einsum('pfok,qwkf->pqwof', banded, padded, precision=lax.Precision.HI...  49.4 us
    dot_general x1, local copies, waits for them, and re-layouts, velocity_whiten(): jnp.einsum('okt,ptf->pfok', shifter, taps, precision=lax.Precision.HIGHEST)  18 us
    dot_general x4, matrix products, cross_block(): jnp.einsum('pwsf,pwcf->scf', source, swapped, preferred_element_type=jnp....  17.4 us
    dot_general x4, matrix products, cross_block(): jnp.einsum('pwsf,pwcf->scf', source, whitened, preferred_element_type=jnp...  17.2 us
    dot_general x1, matrix products, velocity_whiten(): jnp.einsum('okt,ptf->pfok', shifter, taps, precision=lax.Precision.HIGHEST)  8.01 us
  transfers between devices with their start and end apart: 2, of which 0 were waited for; matrix products, arithmetic and copies ran while one was open for 10% of the time, Pallas kernels for 0%

commit v1 on v0

--- a/solution.py
+++ b/solution.py
@@ -9,6 +9,11 @@
 SMOOTH = 17
 ROUNDS = 4
 water_level = 0.05
+
+
+def gather_and_add(value, axis):
+    parts = lax.all_gather(value, axis)
+    return jnp.sum(parts, axis=0)
 
 
 def padded_2(cells, sides, width):
@@ -88,7 +93,7 @@
             for round_pos in range(ROUNDS)
         ]
     )
-    summed = lax.psum(stacked, "chan").astype(jnp.bfloat16)
+    summed = gather_and_add(stacked, "chan").astype(jnp.bfloat16)
     for round_pos in range(ROUNDS):
         blocks.append(cross_block(summed[round_pos], whitened, swapped))
     return jnp.concatenate(blocks, axis=1)

time: 285 us -> 397 us (1.39)
  waiting for transfers between devices: 0.01 us -> 173 us
  blocking collectives: 78.1 us -> 0 us
  between operations: 3.13 us -> 16.5 us
  other arithmetic: 19.4 us -> 31.9 us
  matrix products: 95.1 us -> 84.2 us
    all_gather x0 -> x1, waiting for transfers between devices: none -> 173 us  [gather_and_add(): parts = lax.all_gather(value, axis)]
    psum x1 -> x0, blocking collectives: 78.1 us -> none  [body(): summed = lax.psum(stacked, 'chan').astype(jnp.bfloat16)]
    reduce_sum x0 -> x1, other arithmetic: none -> 12.9 us  [gather_and_add(): return jnp.sum(parts, axis=0)]
    dot_general x1, matrix products: 49.4 us -> 38.2 us  [velocity_whiten(): jnp.einsum('pfok,qwkf->pqwof', banded, padded, precision=lax.Precision.HI...]
    reduce_sum x0 -> x1, local copies, waits for them, and re-layouts: none -> 4.66 us  [gather_and_add(): return jnp.sum(parts, axis=0)]
  transfers between devices with their start and end apart: 2 -> 3, of which waited for: 0 -> 1; matrix products, arithmetic and copies ran while one was open for 10% -> 7% of each run, Pallas kernels for 0% -> 0%
where the time goes in v1:
time: 397 us; the launch traced here: 392 us
  waiting for transfers between devices  173 us (44%)
  matrix products  84.2 us (21%)
  local copies, waits for them, and re-layouts  82.7 us (21%)
  other arithmetic  31.9 us (8%)
  between operations  16.5 us (4%)
    all_gather x1, waiting for transfers between devices, gather_and_add(): parts = lax.all_gather(value, axis)  173 us
    another operation x8, local copies, waits for them, and re-layouts, cross_block(): return (jnp.stack([real_out, imag_out]) / WIN).astype(jnp.bfloat16)  52.2 us
    dot_general x1, matrix products, velocity_whiten(): jnp.einsum('pfok,qwkf->pqwof', banded, padded, precision=lax.Precision.HI...  38.2 us
    dot_general x1, local copies, waits for them, and re-layouts, velocity_whiten(): jnp.einsum('okt,ptf->pfok', shifter, taps, precision=lax.Precision.HIGHEST)  18.1 us
    dot_general x4, matrix products, cross_block(): jnp.einsum('pwsf,pwcf->scf', source, whitened, preferred_element_type=jnp...  17.5 us
    dot_general x4, matrix products, cross_block(): jnp.einsum('pwsf,pwcf->scf', source, swapped, preferred_element_type=jnp....  17.4 us
    reduce_sum x1, other arithmetic, gather_and_add(): return jnp.sum(parts, axis=0)  12.9 us
    dot_general x1, matrix products, velocity_whiten(): jnp.einsum('okt,ptf->pfok', shifter, taps, precision=lax.Precision.HIGHEST)  8 us
  transfers between devices with their start and end apart: 3, of which 1 were waited for; matrix products, arithmetic and copies ran while one was open for 7% of the time, Pallas kernels for 0%

profile of v1, /device:TPU:0, one launch (start us, length us, event | category | flops | bytes accessed | tf_op | source)
XLA Modules:
  0.0 391.9 jit_solution(4462330221985043085)
XLA Ops:
  11.5 8.0 %convolution_bitcast_fusion = f32[2,512,32,96,1]{1,3,2,0,4:T(8,128)} fusion(f32[2,65,512,1]{2,1,3,0:T(8,128)S(1)} %convolution_bitcast_fusion.10, s32[32,96]{1,0:T(8,128)S(1)} %iota_subtract_fusion), kind=kOutput, calls=%fused_computation.1 | convolution fusion | flops 2453867520 | bytes 12861440 | tf_op jit(solution)/shard_map/okt,ptf->pfok/dot_general | solution.py:51
  23.4 18.1 %copy.86 = f32[2,512,32,96,1]{3,2,0,4,1:T(8,128)} copy(f32[2,512,32,96,1]{1,3,2,0,4:T(8,128)} %convolution_bitcast_fusion) | data formatting | bytes 25165824 | tf_op jit(solution)/shard_map/okt,ptf->pfok/dot_general | solution.py:51
  42.9 38.2 %convolution_bitcast_fusion.9 = f32[2,2,4,32,512]{3,2,0,1,4:T(4,128)} fusion(f32[2,512,32,96,1]{3,2,0,4,1:T(8,128)} %copy.86, bf16[2,4,32,512]{2,1,0,3:T(4,128)(2,1)S(1)} %copy.57, bf16[2,4,32,512]{2,1,0,3:T(4,128)(2,1)S(1)} %copy.56, bf16[2,4,32,512]{2,1,0,3:T(4,128)(2,1)S(1)} %copy.55), kind=kOutput, calls=%fused_computation.18 | convolution fusion | flops 304349184 | bytes 14417920 | tf_op jit(solution)/shard_map/pfok,qwkf->pqwof/dot_general | solution.py:52
  93.9 172.8 %all-gather.3.cloned.1.call-done = f32[64,2,4,32,512]{4,3,2,1,0:T(8,128)} async-done(((f32[4,2,4,32,512]{4,3,2,1,0:T(8,128)}), f32[64,2,4,32,512]{4,3,2,1,0:T(8,128)}) %all-gather.3.cloned.1.call-update) | async-done | bytes 33554448 | tf_op jit(solution)/shard_map/all_gather | solution.py:15
  266.7 12.9 %reduce_sum.9 = bf16[4,2,4,32,512]{4,3,2,1,0:T(8,128)(2,1)S(1)} reduce(f32[16,4,2,4,32,512]{5,4,3,2,1,0:T(8,128)} %bitcast.174, f32[]{:T(128)} %constant.17.clone.1), dimensions={0}, to_apply=%region_0.1 | reduce | flops 7864320 | bytes 34603012 | tf_op jit(solution)/shard_map/reduce_sum | solution.py:16
  279.6 4.7 %copy.67 = bf16[4,2,4,32,512]{3,2,1,4,0:T(4,128)(2,1)} copy(bf16[4,2,4,32,512]{4,3,2,1,0:T(8,128)(2,1)S(1)} %reduce_sum.9) | data formatting | bytes 2097152 | tf_op jit(solution)/shard_map/reduce_sum | solution.py:16
  287.2 4.3 %convolution_bitcast_fusion.8 = f32[1,32,32,512]{1,2,3,0:T(8,128)} fusion(bf16[2,4,32,512]{2,1,0,3:T(4,128)(2,1)S(1)} %get-tuple-element.7, bf16[1,4,32,512]{2,1,3,0:T(4,128)(2,1)S(1)} %fusion.40, bf16[1,4,32,512]{2,1,3,0:T(4,128)(2,1)S(1)} %get-tuple-element.6), kind=kOutput, calls=%fused_computation.17 | convolution fusion | flops 8912896 | bytes 2621440 | tf_op jit(solution)/shard_map/pwsf,pwcf->scf/dot_general | solution.py:65
  291.5 4.3 %convolution_bitcast_fusion.7 = f32[1,32,32,512]{1,2,3,0:T(8,128)} fusion(bf16[2,4,32,512]{2,1,0,3:T(4,128)(2,1)S(1)} %get-tuple-element.7, bf16[1,4,32,512]{2,1,3,0:T(4,128)(2,1)S(1)} %get-tuple-element.5, bf16[1,4,32,512]{2,1,3,0:T(4,128)(2,1)S(1)} %fusion.40), kind=kOutput, calls=%fused_computation.16 | convolution fusion | flops 8912896 | bytes 2621440 | tf_op jit(solution)/shard_map/pwsf,pwcf->scf/dot_general | solution.py:66
  295.8 4.5 %convolution_bitcast_fusion.3 = f32[1,32,32,512]{1,2,3,0:T(8,128)} fusion(bf16[2,4,32,512]{2,1,0,3:T(4,128)(2,1)S(1)} %get-tuple-element.8, bf16[1,4,32,512]{2,1,3,0:T(4,128)(2,1)S(1)} %get-tuple-element.5, bf16[1,4,32,512]{2,1,3,0:T(4,128)(2,1)S(1)} %fusion.40), kind=kOutput, calls=%fused_computation.12 | convolution fusion | flops 8912896 | bytes 2621440 | tf_op jit(solution)/shard_map/pwsf,pwcf->scf/dot_general | solution.py:66
  300.3 4.3 %convolution_bitcast_fusion.4 = f32[1,32,32,512]{1,2,3,0:T(8,128)} fusion(bf16[2,4,32,512]{2,1,0,3:T(4,128)(2,1)S(1)} %get-tuple-element.8, bf16[1,4,32,512]{2,1,3,0:T(4,128)(2,1)S(1)} %fusion.40, bf16[1,4,32,512]{2,1,3,0:T(4,128)(2,1)S(1)} %get-tuple-element.6), kind=kOutput, calls=%fused_computation.13 | convolution fusion | flops 8912896 | bytes 2621440 | tf_op jit(solution)/shard_map/pwsf,pwcf->scf/dot_general | solution.py:65
  304.6 4.3 %convolution_bitcast_fusion.5 = f32[1,32,32,512]{1,2,3,0:T(8,128)} fusion(bf16[2,4,32,512]{2,1,0,3:T(4,128)(2,1)S(1)} %get-tuple-element.9, bf16[1,4,32,512]{2,1,3,0:T(4,128)(2,1)S(1)} %get-tuple-element.5, bf16[1,4,32,512]{2,1,3,0:T(4,128)(2,1)S(1)} %fusion.40), kind=kOutput, calls=%fused_computation.14 | convolution fusion | flops 8912896 | bytes 2621440 | tf_op jit(solution)/shard_map/pwsf,pwcf->scf/dot_general | solution.py:66
  308.9 4.3 %convolution_bitcast_fusion.6 = f32[1,32,32,512]{1,2,3,0:T(8,128)} fusion(bf16[2,4,32,512]{2,1,0,3:T(4,128)(2,1)S(1)} %get-tuple-element.9, bf16[1,4,32,512]{2,1,3,0:T(4,128)(2,1)S(1)} %fusion.40, bf16[1,4,32,512]{2,1,3,0:T(4,128)(2,1)S(1)} %get-tuple-element.6), kind=kOutput, calls=%fused_computation.15 | convolution fusion | flops 8912896 | bytes 2621440 | tf_op jit(solution)/shard_map/pwsf,pwcf->scf/dot_general | solution.py:65
  313.2 4.5 %convolution_bitcast_fusion.2 = f32[1,32,32,512]{1,2,3,0:T(8,128)} fusion(bf16[2,4,32,512]{2,1,0,3:T(4,128)(2,1)S(1)} %get-tuple-element.10, bf16[1,4,32,512]{2,1,3,0:T(4,128)(2,1)S(1)} %fusion.40, bf16[1,4,32,512]{2,1,3,0:T(4,128)(2,1)S(1)} %get-tuple-element.6), kind=kOutput, calls=%fused_computation.11 | convolution fusion | flops 8912896 | bytes 2621440 | tf_op jit(solution)/shard_map/pwsf,pwcf->scf/dot_general | solution.py:65
  317.7 4.3 %convolution_bitcast_fusion.1 = f32[1,32,32,512]{1,2,3,0:T(8,128)} fusion(bf16[2,4,32,512]{2,1,0,3:T(4,128)(2,1)S(1)} %get-tuple-element.10, bf16[1,4,32,512]{2,1,3,0:T(4,128)(2,1)S(1)} %get-tuple-element.5, bf16[1,4,32,512]{2,1,3,0:T(4,128)(2,1)S(1)} %fusion.40), kind=kOutput, calls=%fused_computation.10 | convolution fusion | flops 8912896 | bytes 2621440 | tf_op jit(solution)/shard_map/pwsf,pwcf->scf/dot_general | solution.py:66
  322.0 6.6 %copy.71 = f32[1,32,32,512]{3,2,1,0:T(8,128)} copy(f32[1,32,32,512]{1,2,3,0:T(8,128)} %convolution_bitcast_fusion.7) | data formatting | bytes 4194304 | tf_op jit(solution)/shard_map/stack | solution.py:67
  328.6 6.6 %copy.70 = f32[1,32,32,512]{3,2,1,0:T(8,128)} copy(f32[1,32,32,512]{1,2,3,0:T(8,128)} %convolution_bitcast_fusion.8) | data formatting | bytes 4194304 | tf_op jit(solution)/shard_map/stack | solution.py:67
  335.3 5.8 %copy.79 = f32[1,32,32,512]{3,2,1,0:T(8,128)S(1)} copy(f32[1,32,32,512]{1,2,3,0:T(8,128)} %convolution_bitcast_fusion.3) | data formatting | bytes 4194304 | tf_op jit(solution)/shard_map/stack | solution.py:67
  341.1 6.6 %copy.78 = f32[1,32,32,512]{3,2,1,0:T(8,128)} copy(f32[1,32,32,512]{1,2,3,0:T(8,128)} %convolution_bitcast_fusion.4) | data formatting | bytes 4194304 | tf_op jit(solution)/shard_map/stack | solution.py:67
  347.7 6.7 %copy.75 = f32[1,32,32,512]{3,2,1,0:T(8,128)} copy(f32[1,32,32,512]{1,2,3,0:T(8,128)} %convolution_bitcast_fusion.5) | data formatting | bytes 4194304 | tf_op jit(solution)/shard_map/stack | solution.py:67
  354.3 6.6 %copy.74 = f32[1,32,32,512]{3,2,1,0:T(8,128)} copy(f32[1,32,32,512]{1,2,3,0:T(8,128)} %convolution_bitcast_fusion.6) | data formatting | bytes 4194304 | tf_op jit(solution)/shard_map/stack | solution.py:67
  360.9 6.6 %copy.82 = f32[1,32,32,512]{3,2,1,0:T(8,128)} copy(f32[1,32,32,512]{1,2,3,0:T(8,128)} %convolution_bitcast_fusion.2) | data formatting | bytes 4194304 | tf_op jit(solution)/shard_map/stack | solution.py:67
  367.6 6.6 %copy.83 = f32[1,32,32,512]{3,2,1,0:T(8,128)} copy(f32[1,32,32,512]{1,2,3,0:T(8,128)} %convolution_bitcast_fusion.1) | data formatting | bytes 4194304 | tf_op jit(solution)/shard_map/stack | solution.py:67
  374.2 4.2 %fusion = (bf16[2,32,32,512]{3,2,1,0:T(8,128)(2,1)S(1)}, bf16[2,32,32,512]{3,2,1,0:T(8,128)(2,1)S(1)}) fusion(f32[1,32,32,512]{3,2,1,0:T(8,128)} %copy.71, f32[1,32,32,512]{3,2,1,0:T(8,128)} %copy.70, f32[1,32,32,512]{3,2,1,0:T(8,128)} %copy.75, f32[1,32,32,512]{3,2,1,0:T(8,128)} %copy.74), kind=kLoop, calls=%fused_computation.3 | loop fusion | flops 6291456 | bytes 12582912 | tf_op jit(solution)/shard_map/convert_element_type | solution.py:67
  380.9 3.9 pad_maximum_fusion
  (46 shorter events, 25.8 us)
Async XLA Ops:
  6.5 3.9 copy-start
  6.5 260.1 %all-gather.3.cloned.1.call-start = ((), (), s32[]{:S(2)}) async-start(), calls=%async_computation | async-start | bytes 35651584 | tf_op jit(solution)/shard_map/all_gather | solution.py:15
  6.5 35.7 %collective-permute-start = (bf16[2,4,32,512]{3,2,1,0:T(8,128)(2,1)}, bf16[2,4,32,512]{3,2,1,0:T(8,128)(2,1)S(1)}, u32[]{:S(2)}, u32[]{:S(2)}) collective-permute-start(bf16[2,4,32,512]{3,2,1,0:T(8,128)(2,1)} %param.6), channel_id=1, source_target_pairs={{0,1},{1,2},{2,3},{3,4},{4,5},{5,6},{6,7},{7,8},{8,9},{9,10},{10,1... | collective-permute-start | bytes 786440 | tf_op jit(solution)/shard_map/ppermute | solution.py:27
  9.1 32.4 %collective-permute-start.1 = (bf16[2,4,32,512]{3,2,1,0:T(8,128)(2,1)}, bf16[2,4,32,512]{3,2,1,0:T(8,128)(2,1)S(1)}, u32[]{:S(2)}, u32[]{:S(2)}) collective-permute-start(bf16[2,4,32,512]{3,2,1,0:T(8,128)(2,1)} %param.6), channel_id=1, source_target_pairs={{1,0},{2,1},{3,2},{4,3},{5,4},{6,5},{7,6},{8,7},{9,8},{10,9},{11,1... | collective-permute-start | bytes 786440 | tf_op jit(solution)/shard_map/ppermute | solution.py:29
  11.4 8.0 %copy-start.6 = (s32[4]{0:T(128)S(1)}, s32[4]{0:T(128)}, u32[]{:S(2)}) copy-start(s32[4]{0:T(128)} %param.10) | copy-start | bytes 52
  11.4 8.7 %copy-start.5 = (bf16[2,4,32,512]{3,2,1,0:T(8,128)(2,1)S(1)}, bf16[2,4,32,512]{3,2,1,0:T(8,128)(2,1)}, u32[]{:S(2)}) copy-start(bf16[2,4,32,512]{3,2,1,0:T(8,128)(2,1)} %param.6) | copy-start | bytes 786436
  11.4 9.4 %copy-start.7 = (s32[4,32]{1,0:T(4,128)S(1)}, s32[4,32]{1,0:T(4,128)}, u32[]{:S(2)}) copy-start(s32[4,32]{1,0:T(4,128)} %param.9) | copy-start | bytes 1540
  23.4 18.1 %copy-start.8 = (s32[4,32]{1,0:T(4,128)S(1)}, s32[4,32]{1,0:T(4,128)}, u32[]{:S(2)}) copy-start(s32[4,32]{1,0:T(4,128)} %param.11) | copy-start | bytes 1540
  374.2 4.2 %copy-start.2 = (f32[1,32,32,512]{3,2,1,0:T(8,128)S(1)}, f32[1,32,32,512]{3,2,1,0:T(8,128)}, u32[]{:S(2)}) copy-start(f32[1,32,32,512]{3,2,1,0:T(8,128)} %copy.78) | copy-start | bytes 6291460
  374.2 4.7 %copy-start.3 = (f32[1,32,32,512]{3,2,1,0:T(8,128)S(1)}, f32[1,32,32,512]{3,2,1,0:T(8,128)}, u32[]{:S(2)}) copy-start(f32[1,32,32,512]{3,2,1,0:T(8,128)} %copy.82) | copy-start | bytes 6291460
  374.2 5.3 %copy-start.4 = (f32[1,32,32,512]{3,2,1,0:T(8,128)S(1)}, f32[1,32,32,512]{3,2,1,0:T(8,128)}, u32[]{:S(2)}) copy-start(f32[1,32,32,512]{3,2,1,0:T(8,128)} %copy.83) | copy-start | bytes 6291460
  380.9 3.9 copy-start.1
Sparse Core Ops, SparseCore 0:
  94.0 172.6 all-gather.2
